TPU v7x, 32 devices: a whole 2x2x4 slice. The times are simulated.
32 devices in a mesh: blocks: 32 (over z, y, x, core).
Axes of the slice: x: 2, y: 2, z: 4, core: 2. Of those that a mesh axis runs over, the one named last changes fastest.
Arguments:
- spectra: float32 [1152, 66, 512], P('blocks'), may hold values from 0.05 to 2
- courant: float32 [1152, 3, 512], P('blocks'), may hold values from 0.05 to 0.3
- kernel: bfloat16 [66, 4356], replicated, may hold values from -0.09375 to 0.09375
- old_count: int32 [32], replicated, may hold values from 12 to 36, as said below
- new_count: int32 [32], replicated, may hold values from 12 to 36, as said below
- upwind: int32 [768, 3], replicated, may hold values from 0 to 767, as said below
Outputs:
- updated: float32 [1152, 66, 512], P('blocks')
Inputs may be any that keep to these rules, and one draw needn't show every extreme that they name: `old_count`: each count lies in the stated range and both ends are reached in the old and in the new layout; the counts sum to 768; between the two layouts every device boundary along the curve moves by at most 12 blocks, and in every draw some boundary moves by exactly 12 blocks toward higher devices and another by exactly 12 toward lower devices. `new_count`: as old_count, for the new layout. Blocks form aligned runs of 12 along the curve, each run one cross-section of the grid; upwind[b, 0] = b - s * 12 cyclically over 768, where s is +1 or -1 and depends only on b's position within its run, both signs occurring; upwind[b, 1] and upwind[b, 2] lie in the same run as b, arranged alike in every run; every block is upwind of exactly one block per direction.
All inputs are finite; a program needn't handle non-finite values.
Results may differ from a plain program's by a relative error of at most 0.0022.
Values sent between devices are 32-bit elements; how exact they have to be, the bound alone decides.
A program may use at most 128 MiB of HBM per device.

v0:
```python
import functools

import jax
import jax.numpy as jnp
from jax import lax
from jax.experimental import pallas as pl
from jax.experimental.pallas import tpu as pltpu
from jax.sharding import PartitionSpec as P

HALF = 12
BINS = 66
EDGE = 8
CELLS = 512
YZ = 6
PACK = HALF * 64 + 2 * CELLS
ROWS = 72
STRIDES = (64, 8, 1)
KDIM = 2816
VMEM_LIMIT = 63 * 1024 * 1024
CHUNKS = ((0, 16), (16, 32), (32, 48), (48, 64), (64, 66))
F32 = jnp.float32

T_OC, T_NC, T_OS, T_NS = 0, 1, 2, 3
T_SEND = 8
T_SRC = 32


def lane_coord(direction, rows):
    lane = lax.broadcasted_iota(jnp.int32, (rows, CELLS), 1)
    return (lane // STRIDES[direction]) % EDGE


def table_kernel(n, capacity, meta, tab):
    me = meta[0]

    def total(base, count):
        return lax.fori_loop(0, count, lambda i, s: s + meta[base + i], jnp.int32(0))

    old_start, new_start = total(1, me), total(1 + n, me)
    oc, nc = meta[1 + me], meta[1 + n + me]
    tab[T_OC] = oc
    tab[T_NC] = nc
    tab[T_OS] = old_start
    tab[T_NS] = new_start
    base = 1 + 2 * n
    end = old_start + oc
    zero = jnp.int32(0)
    end_run = lax.rem(end, HALF)
    start_run = lax.rem(old_start, HALF)

    def up(t, d):
        return meta[base + 3 * t + d] - HALF

    for d in (1, 2):
        for k in range(YZ):
            tab[T_SEND + (d - 1) * YZ + k] = zero
            tab[T_SEND + 2 * YZ + (d - 1) * YZ + k] = zero

    def block_src(b, carry):
        pos = lax.rem(old_start + b, HALF)
        rel = meta[base + 3 * pos] - HALF - pos
        u = b + rel
        tab[T_SRC + 3 * b] = jnp.where(
            u < 0, capacity + HALF + u, jnp.where(u >= oc, capacity + HALF + u - oc, u)
        )
        for d in (1, 2):
            tab[T_SRC + 3 * b + d] = jnp.clip(b + up(pos, d) - pos, 0, capacity - 1)
        return carry

    lax.fori_loop(0, capacity, block_src, zero)

    for d in (1, 2):
        pool = capacity + 2 * HALF + (d - 1) * 2 * YZ

        def link(t, counts):
            s_up, s_dn, r_up, r_dn = counts
            u = up(t, d)
            cross = (t >= end_run) & (u < end_run)

            @pl.when(cross)
            def _():
                tab[T_SEND + (d - 1) * YZ + s_up] = jnp.clip(oc - end_run + u, 0, capacity - 1)

            s_up = s_up + cross.astype(jnp.int32)
            cross = (t < end_run) & (u >= end_run)
            b = oc - end_run + t

            @pl.when(cross & (b >= 0))
            def _():
                tab[T_SRC + 3 * b + d] = pool + YZ + r_dn

            r_dn = r_dn + cross.astype(jnp.int32)
            cross = (t < start_run) & (u >= start_run)

            @pl.when(cross)
            def _():
                tab[T_SEND + 2 * YZ + (d - 1) * YZ + s_dn] = jnp.clip(
                    u - start_run, 0, capacity - 1
                )

            s_dn = s_dn + cross.astype(jnp.int32)
            cross = (t >= start_run) & (u < start_run)

            @pl.when(cross)
            def _():
                tab[T_SRC + 3 * jnp.minimum(t - start_run, capacity - 1) + d] = pool + r_up

            r_up = r_up + cross.astype(jnp.int32)
            return s_up, s_dn, r_up, r_dn

        lax.fori_loop(0, HALF, link, (zero, zero, zero, zero))


def pack(out, field, tab):
    oc = tab[T_OC]
    for r0, r1 in CHUNKS:
        low = lax.broadcasted_iota(jnp.int32, (r1 - r0, 128), 1) < 64
        coords = [lane_coord(d, r1 - r0) for d in (1, 2)]
        for side in range(2):
            first = oc - HALF if side == 0 else 0
            for j in range(0, HALF, 2):
                a = field(first + j, 0, r0, r1)[:, 384:]
                b = field(first + j + 1, 0, r0, r1)[:, 384:]
                out(side, r0, r1, 64 * j, jnp.where(low, pltpu.roll(a, 64, 1), b))
            for d in (1, 2):
                total = jnp.zeros((r1 - r0, CELLS), F32)
                for k in range(YZ):
                    block = tab[T_SEND + side * 2 * YZ + (d - 1) * YZ + k]
                    value = field(block, d, r0, r1)
                    shift = (CELLS - STRIDES[d] * (EDGE - 1 - k)) % CELLS
                    total = jnp.where(coords[d - 1] == k, pltpu.roll(value, shift, 1), total)
                out(side, r0, r1, HALF * 64 + (d - 1) * CELLS, total)


def unpack(packet, place, capacity):
    for r0, r1 in CHUNKS:
        for side in range(2):
            for j in range(HALF):
                value = packet(side, r0, r1, 128 * (j // 2), 128)
                if j % 2 == 0:
                    value = pltpu.roll(value, 64, 1)
                place(capacity + side * HALF + j, r0, r1, 384, value, 0)
            for d in (1, 2):
                value = packet(side, r0, r1, HALF * 64 + (d - 1) * CELLS, CELLS)
                for k in range(YZ):
                    slot = capacity + 2 * HALF + (d - 1) * 2 * YZ + side * YZ + k
                    place(slot, r0, r1, 0, pltpu.roll(value, STRIDES[d] * (EDGE - 1 - k), 1), d)


def shifted(value, upwind, direction, coord):
    if direction:
        upwind = pltpu.roll(upwind, CELLS - STRIDES[direction - 1], 1)
    return pltpu.roll(jnp.where(coord == EDGE - 1, upwind, value), STRIDES[direction], 1)


def faces_kernel(n, capacity, meta, q0, cs, tab, up, dn):
    table_kernel(n, capacity, meta, tab)
    outs = (up, dn)

    def field(block, d, r0, r1):
        return q0[block, r0:r1, :] * cs[block, d : d + 1, :]

    def out(side, r0, r1, lane, value):
        outs[side][r0:r1, lane : lane + value.shape[1]] = value

    pack(out, field, tab)


def first_kernel(capacity, tab, q0, cs, from_prev, from_next, q1, up, dn, pool):
    packets = (from_prev, from_next)

    def place(slot, r0, r1, l0, value, d):
        pool[slot - capacity, r0:r1, l0 : l0 + value.shape[1]] = value

    unpack(
        lambda side, r0, r1, lane, width: packets[side][r0:r1, lane : lane + width],
        place,
        capacity,
    )

    def step(b, carry):
        srcs = [tab[T_SRC + 3 * b + d] for d in range(3)]
        local = [jnp.minimum(s, capacity - 1) for s in srcs]
        far = [jnp.maximum(s - capacity, 0) for s in srcs]
        remote = [s >= capacity for s in srcs]
        for r0, r1 in CHUNKS:
            q = q0[b, r0:r1, :]
            result = q
            for d in range(3):
                coord = lane_coord(d, r1 - r0)
                flux = q * cs[b, d : d + 1, :]
                near = q0[local[d], r0:r1, :] * cs[local[d], d : d + 1, :]
                upwind = jnp.where(remote[d], pool[far[d], r0:r1, :], near)
                result = result - flux + shifted(flux, upwind, d, coord)
            q1[b, r0:r1, :] = result
        return carry

    lax.fori_loop(0, tab[T_OC], step, 0)

    outs = (up, dn)

    def flux_field(block, d, r0, r1):
        q = q1[block, r0:r1, :]
        c = cs[block, d : d + 1, :]
        m = q - pltpu.roll(q, STRIDES[d], 1)
        m = jnp.maximum(jnp.minimum(m, q), 0.0)
        return c * (q + (0.5 * (1.0 - c)) * m)

    def layer_field(block, d, r0, r1):
        return q1[block, r0:r1, :]

    for part, field in enumerate((flux_field, layer_field)):

        def out(side, r0, r1, lane, value, part=part):
            lane = lane + part * PACK
            outs[side][r0:r1, lane : lane + value.shape[1]] = value

        pack(out, field, tab)


def second_kernel(
    capacity, tab, q1, cs, from_prev, from_next, q2, mig_up, mig_dn, lpool, fx, fy, fz
):
    packets = (from_prev, from_next)
    fluxes = (fx, fy, fz)
    bases = (capacity, capacity + 2 * HALF, capacity + 2 * HALF + 2 * YZ)

    def place_layer(slot, r0, r1, l0, value, d):
        lpool[slot - capacity, r0:r1, l0 : l0 + value.shape[1]] = value

    def place_flux(slot, r0, r1, l0, value, d):
        fluxes[d][slot - bases[d] + capacity, r0:r1, l0 : l0 + value.shape[1]] = value

    for part, place in enumerate((place_flux, place_layer)):
        unpack(
            lambda side, r0, r1, lane, width, part=part: packets[side][
                r0:r1, part * PACK + lane : part * PACK + lane + width
            ],
            place,
            capacity,
        )

    def limit(b, carry):
        for d in range(3):
            src = tab[T_SRC + 3 * b + d]
            local = jnp.minimum(src, capacity - 1)
            far = jnp.maximum(src - capacity, 0)
            remote = src >= capacity
            c = cs[b, d : d + 1, :]
            half = 0.5 * (1.0 - c)
            for r0, r1 in CHUNKS:
                coord = lane_coord(d, r1 - r0)
                q = q1[b, r0:r1, :]
                upwind = jnp.where(remote, lpool[far, r0:r1, :], q1[local, r0:r1, :])
                m = q - shifted(q, upwind, d, coord)
                m = jnp.maximum(jnp.minimum(m, q), 0.0)
                fluxes[d][b, r0:r1, :] = c * (q + half * m)
        return carry

    lax.fori_loop(0, tab[T_OC], limit, 0)

    def step(b, carry):
        srcs = [tab[T_SRC + 3 * b + d] for d in range(3)]
        srcs = [
            jnp.where(srcs[d] >= capacity, srcs[d] - bases[d] + capacity, srcs[d])
            for d in range(3)
        ]
        for r0, r1 in CHUNKS:
            result = q1[b, r0:r1, :]
            for d in range(3):
                coord = lane_coord(d, r1 - r0)
                flux = fluxes[d][b, r0:r1, :]
                upwind = fluxes[d][srcs[d], r0:r1, :]
                result = result - flux + shifted(flux, upwind, d, coord)
            q2[b, r0:r1, :] = result
        return carry

    oc = tab[T_OC]
    lax.fori_loop(0, oc, step, 0)

    def copy(j, carry):
        mig_up[j] = q2[oc - HALF + j]
        mig_dn[j] = q2[j]
        return carry

    lax.fori_loop(0, HALF, copy, 0)


def build_pairs(q, qp, pairs):
    qp[0:BINS, :] = q
    qp[BINS : BINS + 1, :] = q[BINS - 1 : BINS, :]
    qp[BINS + 1 : BINS + 2, :] = q[BINS - 2 : BINS - 1, :]
    qp[BINS + 2 : ROWS, :] = jnp.zeros((ROWS - BINS - 2, CELLS), F32)
    row = lax.broadcasted_iota(jnp.int32, (8, CELLS), 0)
    pending = None
    at = 0
    for i in range(BINS - 2):
        lead = jnp.broadcast_to(qp[i : i + 1, :], (8, CELLS))
        for g in range(i // 8, ROWS // 8):
            by = lead
            if i < 2 and g == ROWS // 8 - 1:
                by = jnp.where(row < 2, lead, qp[BINS - 1 - i : BINS - i, :])
            term = by * qp[8 * g : 8 * g + 8, :]
            if pending is None:
                pending = term
            else:
                tile = jnp.concatenate([pending, term], axis=0)
                pairs[at : at + 16, :] = tile.astype(jnp.bfloat16)
                pending = None
                at += 16


def coalesce_range(lo, hi, load, w, out, qps, pairs, res, sems):
    def copy_out(slot, buf):
        return pltpu.make_async_copy(res.at[buf], out.at[slot], sems.at[buf])

    count = hi - lo

    def body(it, carry):
        first = lo + 2 * it
        slots = (first, jnp.minimum(first + 1, hi - 1))
        values = [load(s) for s in slots]

        @pl.when(it > 0)
        def _():
            for buf in range(2):
                copy_out(lo, buf).wait()

        for buf in range(2):
            build_pairs(values[buf], qps[buf], pairs[buf])
        for buf in range(2):
            gain = jnp.dot(w[...], pairs[buf][...], preferred_element_type=F32)
            res[buf] = qps[buf][0:BINS, :] + gain
        copy_out(slots[0], 0).start()

        @pl.when(first + 1 < hi)
        def _():
            copy_out(slots[1], 1).start()

        return carry

    trips = lax.div(count + 1, 2)
    lax.fori_loop(0, trips, body, 0)

    @pl.when(trips > 0)
    def _():
        copy_out(lo, 0).wait()

    @pl.when((trips > 0) & (lax.rem(count, 2) == 0))
    def _():
        copy_out(lo, 1).wait()


def stay_kernel(capacity, tab, q2, w, out, qpa, qpb, pa, pb, res, zero, sems, zsem):
    oc, nc, old, new = tab[T_OC], tab[T_NC], tab[T_OS], tab[T_NS]
    zero[...] = jnp.zeros_like(zero)

    def blank(slot):
        return pltpu.make_async_copy(zero, out.at[slot], zsem)

    def start(slot, carry):
        blank(slot).start()
        return carry

    def wait(slot, carry):
        blank(slot).wait()
        return carry

    lax.fori_loop(nc, capacity, start, 0)
    lo = jnp.clip(old - new, 0, nc)
    hi = jnp.clip(old + oc - new, lo, nc)
    coalesce_range(
        lo, hi, lambda s: q2[s + new - old], w, out, (qpa, qpb), (pa, pb), res, sems
    )
    lax.fori_loop(nc, capacity, wait, 0)


def come_kernel(capacity, tab, from_prev, from_next, w, old_out, out, qpa, qpb, pa, pb, res, sems):
    oc, nc, old, new = tab[T_OC], tab[T_NC], tab[T_OS], tab[T_NS]
    args = (w, out, (qpa, qpb), (pa, pb), res, sems)
    coalesce_range(
        jnp.int32(0),
        jnp.clip(old - new, 0, nc),
        lambda s: from_prev[s + new - old + HALF],
        *args,
    )
    coalesce_range(
        jnp.clip(old + oc - new, 0, nc),
        nc,
        lambda s: from_next[s + new - old - oc],
        *args,
    )


def folded_kernel(kernel):
    cube = kernel.reshape(BINS, BINS, BINS).astype(F32)
    turned = jnp.swapaxes(cube, 1, 2)
    i = lax.broadcasted_iota(jnp.int32, cube.shape, 1)
    j = lax.broadcasted_iota(jnp.int32, cube.shape, 2)
    folded = jnp.where(i < j, cube + turned, jnp.where(i == j, cube, 0.0))
    a, b = BINS - 2, BINS - 1
    extra = jnp.zeros((BINS, BINS, ROWS - BINS), F32)
    extra = extra.at[:, 0, 0].set(cube[:, b, b])
    extra = extra.at[:, 1, 0].set(cube[:, a, b] + cube[:, b, a])
    extra = extra.at[:, 1, 1].set(cube[:, a, a])
    wide = jnp.concatenate([folded, extra], axis=2).astype(jnp.bfloat16)
    parts = [
        wide[:, 8 * c : 8 * c + 8, 8 * c :].reshape(BINS, -1) for c in range(BINS // 8)
    ]
    return jnp.concatenate(parts, axis=1)


def on_device(n, spectra, courant, kernel, old_count, new_count, upwind):
    capacity = spectra.shape[0]
    shape = jax.ShapeDtypeStruct
    vmem = pl.BlockSpec(memory_space=pltpu.VMEM)
    smem = pl.BlockSpec(memory_space=pltpu.SMEM)
    hbm = pl.BlockSpec(memory_space=pl.ANY)
    params = pltpu.CompilerParams(vmem_limit_bytes=VMEM_LIMIT)
    blocks = shape((capacity, BINS, CELLS), F32)
    half = shape((HALF, BINS, CELLS), F32)

    def cost(flops, nbytes):
        return pl.CostEstimate(flops=flops, bytes_accessed=nbytes, transcendentals=0)

    meta = jnp.concatenate(
        [
            lax.axis_index("blocks").astype(jnp.int32)[None],
            old_count,
            new_count,
            upwind[HALF : 2 * HALF].reshape(-1),
        ]
    )
    tab, up, dn = pl.pallas_call(
        functools.partial(faces_kernel, n, capacity),
        out_shape=(
            shape((T_SRC + 3 * capacity,), jnp.int32),
            shape((BINS, PACK), F32),
            shape((BINS, PACK), F32),
        ),
        in_specs=[smem, vmem, vmem],
        out_specs=(smem, vmem, vmem),
        compiler_params=params,
        name="faces",
    )(meta, spectra, courant)

    def along(value, step, ring):
        route = [(i, i + step) for i in range(n)]
        if ring:
            route = [(i, j % n) for i, j in route]
        return lax.ppermute(value, "blocks", [(i, j) for i, j in route if 0 <= j < n])

    from_prev, from_next = along(up, 1, True), along(dn, -1, True)
    weights = folded_kernel(kernel)
    q1, up, dn = pl.pallas_call(
        functools.partial(first_kernel, capacity),
        out_shape=(blocks, shape((BINS, 2 * PACK), F32), shape((BINS, 2 * PACK), F32)),
        in_specs=[smem, vmem, vmem, vmem, vmem],
        out_specs=(vmem, vmem, vmem),
        scratch_shapes=[pltpu.VMEM((2 * HALF + 4 * YZ, BINS, CELLS), F32)],
        compiler_params=params,
        name="first",
    )(tab, spectra, courant, from_prev, from_next)
    from_prev, from_next = along(up, 1, True), along(dn, -1, True)
    q1, weights = lax.optimization_barrier((q1, weights))
    q2, up, dn = pl.pallas_call(
        functools.partial(second_kernel, capacity),
        out_shape=(blocks, half, half),
        in_specs=[smem, vmem, vmem, vmem, vmem],
        out_specs=(vmem, vmem, vmem),
        scratch_shapes=[
            pltpu.VMEM((2 * HALF + 4 * YZ, BINS, CELLS), F32),
            pltpu.VMEM((capacity + 2 * HALF, BINS, CELLS), F32),
            pltpu.VMEM((capacity + 2 * YZ, BINS, CELLS), F32),
            pltpu.VMEM((capacity + 2 * YZ, BINS, CELLS), F32),
        ],
        compiler_params=params,
        name="second",
    )(tab, q1, courant, from_prev, from_next)
    from_prev, from_next = along(up, 1, False), along(dn, -1, False)
    buffers = [
        pltpu.VMEM((ROWS, CELLS), F32),
        pltpu.VMEM((ROWS, CELLS), F32),
        pltpu.VMEM((KDIM, CELLS), jnp.bfloat16),
        pltpu.VMEM((KDIM, CELLS), jnp.bfloat16),
        pltpu.VMEM((2, BINS, CELLS), F32),
    ]
    work = 2 * BINS * KDIM * CELLS
    updated = pl.pallas_call(
        functools.partial(stay_kernel, capacity),
        out_shape=blocks,
        in_specs=[smem, vmem, vmem],
        out_specs=hbm,
        scratch_shapes=buffers
        + [
            pltpu.VMEM((BINS, CELLS), F32),
            pltpu.SemaphoreType.DMA((2,)),
            pltpu.SemaphoreType.DMA,
        ],
        compiler_params=params,
        cost_estimate=cost(24 * work, 12 * 1024 * 1024),
        name="stay",
    )(tab, q2, weights)
    return pl.pallas_call(
        functools.partial(come_kernel, capacity),
        out_shape=blocks,
        in_specs=[smem, vmem, vmem, vmem, hbm],
        out_specs=hbm,
        input_output_aliases={4: 0},
        scratch_shapes=buffers + [pltpu.SemaphoreType.DMA((2,))],
        compiler_params=params,
        cost_estimate=cost(12 * work, 6 * 1024 * 1024),
        name="come",
    )(tab, from_prev, from_next, weights, updated)


def solution(mesh):
    in_specs = (P("blocks", None, None), P("blocks", None, None), P(), P(), P(), P())
    out_specs = P("blocks", None, None)
    return jax.shard_map(
        functools.partial(on_device, mesh.shape["blocks"]),
        mesh=mesh,
        in_specs=in_specs,
        out_specs=out_specs,
        check_vma=False,
    )
```

profile of v0, /device:TPU:4, one launch (start us, length us, event | category | flops | bytes accessed | tf_op | source)
XLA Modules:
  0.0 187.8 jit_solution(5320054916911968248)
XLA Ops:
  0.0 0.8 slice.100
  0.8 0.1 copy.13
  0.9 0.1 reshape.120
  0.9 1.8 copy.14.cs
  2.8 1.3 pad_add_fusion.meta
  4.1 0.0 copy-start.1
  4.1 6.1 %faces.1 = (s32[140]{0:T(256)}, f32[66,1792]{1,0:T(8,128)}, f32[66,1792]{1,0:T(8,128)}) custom-call(s32[101]{0:T(128)} %pad_add_fusion.meta, f32[36,66,512]{2,1,0:T(8,128)} %q0.3, f32[36,3,512]{2,1,0:T(4,128)} %copy.14.cs), custom_call_target="tpu_custom_call" | custom-call | tf_op jit(solution)/shard_map/faces/pallas_call | solution.py:434
  10.2 0.1 collective-permute-start
  10.3 2.6 %collective-permute-start.1 = (f32[66,1792]{1,0:T(8,128)}, f32[66,1792]{1,0:T(8,128)}, u32[]{:S(2)}, u32[]{:S(2)}) collective-permute-start(f32[66,1792]{1,0:T(8,128)} %get-tuple-element.54), channel_id=1, source_target_pairs={{0,31},{1,0},{2,1},{3,2},{4,3},{5,4},{6,5},{7,6},{8,7},{9,8},{10,9... | collective-permute-start | bytes 1419272 | tf_op jit(solution)/shard_map/ppermute | solution.py:451
  12.9 0.0 copy-done.1
  12.9 1.1 reshape.129
  14.0 2.2 %copy.17 = f32[66,66,66]{0,2,1:T(8,128)} copy(f32[66,66,66]{2,1,0:T(8,128)S(1)} %reshape.129) | data formatting | bytes 2299968 | tf_op jit(solution)/shard_map/convert_element_type | solution.py:396
  16.2 2.3 %copy.16 = f32[66,66,66]{0,1,2:T(8,128)} copy(f32[66,66,66]{2,1,0:T(8,128)S(1)} %reshape.129) | data formatting | bytes 2299968 | tf_op jit(solution)/shard_map/convert_element_type | solution.py:396
  18.5 3.7 %fusion.1 = bf16[66,66,66]{0,2,1:T(8,128)(2,1)} fusion(f32[66,66,66]{0,2,1:T(8,128)} %copy.17, f32[66,66,66]{0,1,2:T(8,128)} %copy.16), kind=kLoop, calls=%fused_computation.2 | loop fusion | flops 1724976 | bytes 2874960 | tf_op jit(solution)/shard_map/convert.1
  22.2 2.5 %collective-permute-done.from_prev = f32[66,1792]{1,0:T(8,128)} collective-permute-done((f32[66,1792]{1,0:T(8,128)}, f32[66,1792]{1,0:T(8,128)}, u32[]{:S(2)}, u32[]{:S(2)}) %collective-permute-start) | collective-permute-done | bytes 473120 | tf_op jit(solution)/shard_map/ppermute | solution.py:451
  24.7 0.0 collective-permute-done.1.from_next
  24.7 28.2 %first.1 = (f32[36,66,512]{2,1,0:T(8,128)}, f32[66,3584]{1,0:T(8,128)}, f32[66,3584]{1,0:T(8,128)}) custom-call(s32[140]{0:T(256)} %get-tuple-element.52.tab, f32[36,66,512]{2,1,0:T(8,128)} %q0.3, f32[36,3,512]{2,1,0:T(4,128)} %copy.14.cs, f32[66,1792]{1,0:T(8,128)} %collective-permute-done.from_prev, f32[66,1792]{1,0:T(8,128)} %collective-permute-done.1.from_next), custom_call_target="tpu_custom_call" | custom-call | tf_op jit(solution)/shard_map/first/pallas_call | solution.py:455
  52.9 0.0 copy-start
  52.9 10.2 %collective-permute-start.2 = (f32[66,3584]{1,0:T(8,128)}, f32[66,3584]{1,0:T(8,128)}, u32[]{:S(2)}, u32[]{:S(2)}) collective-permute-start(f32[66,3584]{1,0:T(8,128)} %get-tuple-element.57), channel_id=1, source_target_pairs={{0,1},{1,2},{2,3},{3,4},{4,5},{5,6},{6,7},{7,8},{8,9},{9,10},{10,1... | collective-permute-start | bytes 2838536 | tf_op jit(solution)/shard_map/ppermute | solution.py:451
  63.1 0.0 collective-permute-start.3
  63.1 0.8 fusion.2
  63.9 0.2 scatter.14
  64.1 0.8 pad_maximum_fusion.7
  64.9 0.1 copy.30
  65.0 0.8 pad_maximum_fusion.6
  65.8 0.1 copy.29
  65.9 0.0 copy-done
  66.0 0.1 copy.28
  66.1 0.1 copy.27
  66.3 0.1 copy.35
  66.5 0.1 copy.34
  66.6 0.2 copy.32
  66.8 0.1 copy.33
  67.0 1.0 concatenate.19.w
  67.9 12.8 %collective-permute-done.2.from_prev = f32[66,3584]{1,0:T(8,128)} collective-permute-done((f32[66,3584]{1,0:T(8,128)}, f32[66,3584]{1,0:T(8,128)}, u32[]{:S(2)}, u32[]{:S(2)}) %collective-permute-start.2) | collective-permute-done | bytes 946208 | tf_op jit(solution)/shard_map/ppermute | solution.py:451
  80.8 5.1 %collective-permute-done.3.from_next = f32[66,3584]{1,0:T(8,128)} collective-permute-done((f32[66,3584]{1,0:T(8,128)}, f32[66,3584]{1,0:T(8,128)}, u32[]{:S(2)}, u32[]{:S(2)}) %collective-permute-start.3) | collective-permute-done | bytes 946208 | tf_op jit(solution)/shard_map/ppermute | solution.py:451
  85.9 20.6 %second.1 = (f32[36,66,512]{2,1,0:T(8,128)}, f32[12,66,512]{2,1,0:T(8,128)}, f32[12,66,512]{2,1,0:T(8,128)}) custom-call(s32[140]{0:T(256)} %get-tuple-element.52.tab, f32[36,66,512]{2,1,0:T(8,128)} %get-tuple-element.56.q1, f32[36,3,512]{2,1,0:T(4,128)} %copy.14.cs, f32[66,3584]{1,0:T(8,128)} %collective-permute-done.2.from_prev, ...), custom_call_target="tpu_custom_call" | custom-call | tf_op jit(solution)/shard_map/second/pallas_call | solution.py:466
  106.5 19.9 %collective-permute-start.4 = (f32[12,66,512]{2,1,0:T(8,128)}, f32[12,66,512]{2,1,0:T(8,128)}, u32[]{:S(2)}, u32[]{:S(2)}) collective-permute-start(f32[12,66,512]{2,1,0:T(8,128)} %get-tuple-element.59), channel_id=1, source_target_pairs={{0,1},{1,2},{2,3},{3,4},{4,5},{5,6},{6,7},{7,8},{8,9},{9,10},{10,1... | collective-permute-start | bytes 4866056 | tf_op jit(solution)/shard_map/ppermute | solution.py:451
  126.4 1.9 %collective-permute-start.5 = (f32[12,66,512]{2,1,0:T(8,128)}, f32[12,66,512]{2,1,0:T(8,128)}, u32[]{:S(2)}, u32[]{:S(2)}) collective-permute-start(f32[12,66,512]{2,1,0:T(8,128)} %get-tuple-element.60), channel_id=1, source_target_pairs={{1,0},{2,1},{3,2},{4,3},{5,4},{6,5},{7,6},{8,7},{9,8},{10,9},{11,1... | collective-permute-start | bytes 4866056 | tf_op jit(solution)/shard_map/ppermute | solution.py:451
  128.3 15.6 %stay.1.old_out = f32[36,66,512]{2,1,0:T(8,128)} custom-call(s32[140]{0:T(256)} %get-tuple-element.52.tab, f32[36,66,512]{2,1,0:T(8,128)} %get-tuple-element.62.q2, bf16[66,2816]{1,0:T(8,128)(2,1)} %concatenate.19.w), custom_call_target="tpu_custom_call" | custom-call | flops 4567597056 | bytes 12582912 | tf_op jit(solution)/shard_map/stay/pallas_call | solution.py:489
  143.9 13.9 %collective-permute-done.4.from_prev = f32[12,66,512]{2,1,0:T(8,128)} collective-permute-done((f32[12,66,512]{2,1,0:T(8,128)}, f32[12,66,512]{2,1,0:T(8,128)}, u32[]{:S(2)}, u32[]{:S(2)}) %collective-permute-start.4) | collective-permute-done | bytes 1622048 | tf_op jit(solution)/shard_map/ppermute | solution.py:451
  157.8 7.2 %collective-permute-done.5.from_next = f32[12,66,512]{2,1,0:T(8,128)} collective-permute-done((f32[12,66,512]{2,1,0:T(8,128)}, f32[12,66,512]{2,1,0:T(8,128)}, u32[]{:S(2)}, u32[]{:S(2)}) %collective-permute-start.5) | collective-permute-done | bytes 1622048 | tf_op jit(solution)/shard_map/ppermute | solution.py:451
  165.0 22.6 %come.1 = f32[36,66,512]{2,1,0:T(8,128)} custom-call(s32[140]{0:T(256)} %get-tuple-element.52.tab, f32[12,66,512]{2,1,0:T(8,128)} %collective-permute-done.4.from_prev, f32[12,66,512]{2,1,0:T(8,128)} %collective-permute-done.5.from_next, bf16[66,2816]{1,0:T(8,128)(2,1)} %concatenate.19.w, f32[36,66,512]{2,1,0:T(8,128)} %stay.1.old_out), custom_call_target="tpu_custom_call", output_to_operand_aliasing={{}: (4, {})} | custom-call | flops 2283798528 | bytes 6291456 | tf_op jit(solution)/shard_map/come/pallas_call | solution.py:504
  (8 shorter events, 0.3 us)
Async XLA Ops:
  4.1 8.8 %copy-start.1 = (bf16[66,4356]{1,0:T(8,128)(2,1)S(1)}, bf16[66,4356]{1,0:T(8,128)(2,1)}, u32[]{:S(2)}) copy-start(bf16[66,4356]{1,0:T(8,128)(2,1)} %param.14) | copy-start | bytes 1724980
  10.2 14.5 %collective-permute-start = (f32[66,1792]{1,0:T(8,128)}, f32[66,1792]{1,0:T(8,128)}, u32[]{:S(2)}, u32[]{:S(2)}) collective-permute-start(f32[66,1792]{1,0:T(8,128)} %get-tuple-element.53), channel_id=1, source_target_pairs={{0,1},{1,2},{2,3},{3,4},{4,5},{5,6},{6,7},{7,8},{8,9},{9,10},{10,1... | collective-permute-start | bytes 1419272 | tf_op jit(solution)/shard_map/ppermute | solution.py:451
  10.3 14.4 %collective-permute-start.1 = (f32[66,1792]{1,0:T(8,128)}, f32[66,1792]{1,0:T(8,128)}, u32[]{:S(2)}, u32[]{:S(2)}) collective-permute-start(f32[66,1792]{1,0:T(8,128)} %get-tuple-element.54), channel_id=1, source_target_pairs={{0,31},{1,0},{2,1},{3,2},{4,3},{5,4},{6,5},{7,6},{8,7},{9,8},{10,9... | collective-permute-start | bytes 1419272 | tf_op jit(solution)/shard_map/ppermute | solution.py:451
  52.9 13.0 %copy-start = (bf16[66,66,66]{0,2,1:T(8,128)(2,1)S(1)}, bf16[66,66,66]{0,2,1:T(8,128)(2,1)}, u32[]{:S(2)}) copy-start(bf16[66,66,66]{0,2,1:T(8,128)(2,1)} %fusion.1) | copy-start | bytes 1724980
  52.9 27.9 %collective-permute-start.2 = (f32[66,3584]{1,0:T(8,128)}, f32[66,3584]{1,0:T(8,128)}, u32[]{:S(2)}, u32[]{:S(2)}) collective-permute-start(f32[66,3584]{1,0:T(8,128)} %get-tuple-element.57), channel_id=1, source_target_pairs={{0,1},{1,2},{2,3},{3,4},{4,5},{5,6},{6,7},{7,8},{8,9},{9,10},{10,1... | collective-permute-start | bytes 2838536 | tf_op jit(solution)/shard_map/ppermute | solution.py:451
  63.1 22.8 %collective-permute-start.3 = (f32[66,3584]{1,0:T(8,128)}, f32[66,3584]{1,0:T(8,128)}, u32[]{:S(2)}, u32[]{:S(2)}) collective-permute-start(f32[66,3584]{1,0:T(8,128)} %get-tuple-element.58), channel_id=1, source_target_pairs={{0,31},{1,0},{2,1},{3,2},{4,3},{5,4},{6,5},{7,6},{8,7},{9,8},{10,9... | collective-permute-start | bytes 2838536 | tf_op jit(solution)/shard_map/ppermute | solution.py:451
  106.5 51.3 %collective-permute-start.4 = (f32[12,66,512]{2,1,0:T(8,128)}, f32[12,66,512]{2,1,0:T(8,128)}, u32[]{:S(2)}, u32[]{:S(2)}) collective-permute-start(f32[12,66,512]{2,1,0:T(8,128)} %get-tuple-element.59), channel_id=1, source_target_pairs={{0,1},{1,2},{2,3},{3,4},{4,5},{5,6},{6,7},{7,8},{8,9},{9,10},{10,1... | collective-permute-start | bytes 4866056 | tf_op jit(solution)/shard_map/ppermute | solution.py:451
  126.4 38.6 %collective-permute-start.5 = (f32[12,66,512]{2,1,0:T(8,128)}, f32[12,66,512]{2,1,0:T(8,128)}, u32[]{:S(2)}, u32[]{:S(2)}) collective-permute-start(f32[12,66,512]{2,1,0:T(8,128)} %get-tuple-element.60), channel_id=1, source_target_pairs={{1,0},{2,1},{3,2},{4,3},{5,4},{6,5},{7,6},{8,7},{9,8},{10,9},{11,1... | collective-permute-start | bytes 4866056 | tf_op jit(solution)/shard_map/ppermute | solution.py:451
where the time goes:
time: 191 us; the launch traced here: 188 us
  Pallas kernels  93.1 us (49%)
  waiting for transfers between devices  41.6 us (22%)
  starting transfers between devices  34.6 us (18%)
  local copies, waits for them, and re-layouts  10.5 us (5%)
  other arithmetic  7.63 us (4%)
    ppermute x6, waiting for transfers between devices, along(): lax.ppermute(value, 'blocks', [(i, j) for i, j in route if 0 <= j < n])  41.6 us
    ppermute x6, starting transfers between devices, along(): lax.ppermute(value, 'blocks', [(i, j) for i, j in route if 0 <= j < n])  34.6 us
    pallas_call x1, Pallas kernels, on_device(): pl.pallas_call(functools.partial(first_kernel, capacity), out_shape=(bloc...  28.2 us
    pallas_call x1, Pallas kernels, on_device(): pl.pallas_call(functools.partial(come_kernel, capacity), out_shape=blocks...  22.6 us
    pallas_call x1, Pallas kernels, on_device(): pl.pallas_call(functools.partial(second_kernel, capacity), out_shape=(blo...  20.6 us
    pallas_call x1, Pallas kernels, on_device(): pl.pallas_call(functools.partial(stay_kernel, capacity), out_shape=blocks...  15.6 us
    pallas_call x1, Pallas kernels, on_device(): pl.pallas_call(functools.partial(faces_kernel, n, capacity), out_shape=(s...  6.11 us
    convert_element_type x3, local copies, waits for them, and re-layouts, folded_kernel(): cube = kernel.reshape(BINS, BINS, BINS).astype(F32)  5.58 us
  transfers between devices with their start and end apart: 6, of which 5 were waited for; matrix products, arithmetic and copies ran while one was open for 7% of the time, Pallas kernels for 8%

commit v1 on v0

v1 whole, which is shorter than its diff:
```python
import functools

import jax
import jax.numpy as jnp
from jax import lax
from jax.experimental import pallas as pl
from jax.experimental.pallas import tpu as pltpu
from jax.sharding import PartitionSpec as P

HALF = 12
BINS = 66
EDGE = 8
CELLS = 512
TILE = 128
TILES = CELLS // TILE
YZ = 6
XFACES = HALF * 64
PACK = XFACES + 2 * CELLS
EXTRA = 8
ROWS = 72
GROUPS = 288
KDIM = 8 * GROUPS
CHUNK = 4
STRIDES = (64, 8, 1)
ROWSETS = ((0, 32), (32, 64), (64, 66))
VMEM_LIMIT = 63 * 1024 * 1024
F32 = jnp.float32

T_OC, T_NC, T_OS, T_NS = 0, 1, 2, 3
T_SRC = 8
S_COUNT = 0
S_LIST = 8


def position(n, old, new):
    me = lax.axis_index("blocks")

    def total(ref):
        return lax.fori_loop(0, me, lambda i, s: s + ref[i], jnp.int32(0))

    return total(old), total(new), old[me], new[me]


def lane_coord(direction):
    lane = lax.broadcasted_iota(jnp.int32, (1, TILE), 1)
    return (lane // STRIDES[direction]) % EDGE


def low_half():
    return lax.broadcasted_iota(jnp.int32, (1, TILE), 1) < 64


def send_table(capacity, old_start, oc, up, sends):
    zero = jnp.int32(0)
    end_run = lax.rem(old_start + oc, HALF)
    start_run = lax.rem(old_start, HALF)
    for d in (1, 2):

        def link(t, counts):
            s_up, s_dn = counts
            u = up[d, HALF + t] - HALF
            cross = (t >= end_run) & (u < end_run)

            @pl.when(cross)
            def _():
                sends[S_LIST + (d - 1) * 8 + s_up] = jnp.clip(oc - end_run + u, 0, capacity - 1)

            s_up = s_up + cross.astype(jnp.int32)
            cross = (t < start_run) & (u >= start_run)

            @pl.when(cross)
            def _():
                sends[S_LIST + 16 + (d - 1) * 8 + s_dn] = jnp.clip(u - start_run, 0, capacity - 1)

            return s_up, s_dn + cross.astype(jnp.int32)

        s_up, s_dn = lax.fori_loop(0, HALF, link, (zero, zero))
        sends[S_COUNT + d - 1] = jnp.minimum(s_up, YZ)
        sends[S_COUNT + 2 + d - 1] = jnp.minimum(s_dn, YZ)


def plan_kernel(n, capacity, sends, old, new, up, tab):
    old_start, new_start, oc, nc = position(n, old, new)
    tab[T_OC] = oc
    tab[T_NC] = nc
    tab[T_OS] = old_start
    tab[T_NS] = new_start
    tab[T_OC + 4] = sends[S_COUNT]
    end_run = lax.rem(old_start + oc, HALF)
    start_run = lax.rem(old_start, HALF)
    zero = jnp.int32(0)

    def block_src(b, pos):
        at = T_SRC + 8 * b
        u = b + up[0, HALF + pos] - HALF - pos
        above = u >= oc
        remote = above | (u < 0)
        j = jnp.where(above, u - oc, u + HALF)
        base = capacity + jnp.where(above, 4, 0)
        tab[at] = jnp.where(remote, base + (j >> 3), u)
        tab[at + 1] = jnp.where(remote, ((j & 7) >> 1) * TILE, CELLS - TILE)
        tab[at + 2] = jnp.where(remote & ((j & 1) == 0), 64, 0)
        for d in (1, 2):
            tab[at + 1 + 2 * d] = jnp.clip(b + up[d, HALF + pos] - HALF - pos, 0, capacity - 1)
            tab[at + 2 + 2 * d] = TILE - STRIDES[d] * (EDGE - 1)
        return jnp.where(pos == HALF - 1, 0, pos + 1)

    lax.fori_loop(0, capacity, block_src, start_run)

    for d in (1, 2):

        def link(t, counts):
            r_up, r_dn = counts
            u = up[d, HALF + t] - HALF

            def put(b, side, k):
                at = T_SRC + 8 * jnp.clip(b, 0, capacity - 1) + 1 + 2 * d
                tab[at] = capacity + 4 * side + 1 + d
                tab[at + 1] = (TILE - STRIDES[d] * k) & (TILE - 1)

            cross = (t < end_run) & (u >= end_run)

            @pl.when(cross)
            def _():
                put(oc - end_run + t, 1, r_dn)

            r_dn = r_dn + cross.astype(jnp.int32)
            cross = (t >= start_run) & (u < start_run)

            @pl.when(cross)
            def _():
                put(t - start_run, 0, r_up)

            return r_up + cross.astype(jnp.int32), r_dn

        lax.fori_loop(0, HALF, link, (zero, zero))


def pack(oc, sends, field, outs):
    low = low_half()
    coords = [lane_coord(d) for d in range(3)]
    last = pl.ds(CELLS - TILE, TILE)

    def faces(jp, carry):
        for side in range(2):
            first = (oc - HALF if side == 0 else 0) + 2 * jp
            a = field(first, 0, last)
            b = field(first + 1, 0, last)
            for part in range(len(a)):
                lane = pl.multiple_of(part * PACK + jp * TILE, TILE)
                outs[side][:, pl.ds(lane, TILE)] = jnp.where(low, pltpu.roll(a[part], 64, 1), b[part])
        return carry

    lax.fori_loop(0, HALF // 2, faces, 0)
    for side in range(2):
        for d in (1, 2):

            def cross(k, carry, side=side, d=d):
                block = sends[S_LIST + side * 16 + (d - 1) * 8 + k]
                shift = TILE - STRIDES[d] * (EDGE - 1) + STRIDES[d] * k
                for t in range(TILES):
                    values = field(block, d, pl.ds(t * TILE, TILE))
                    for part, value in enumerate(values):
                        lane = part * PACK + XFACES + (d - 1) * CELLS + t * TILE
                        at = pl.ds(lane, TILE)
                        keep = outs[side][:, at]
                        outs[side][:, at] = jnp.where(coords[d] == k, pltpu.roll(value, shift, 1), keep)
                return carry

            lax.fori_loop(0, sends[S_COUNT + side * 2 + d - 1], cross, 0)


def faces_kernel(n, capacity, old, new, upw, q0, speeds, sends, up, dn, cs):
    old_start, _, oc, _ = position(n, old, new)
    send_table(capacity, old_start, oc, upw, sends)
    for b0 in range(0, capacity, 8):
        b1 = min(b0 + 8, capacity)
        for t in range(TILES):
            at = pl.ds(t * TILE, TILE)
            cs[b0:b1, :, at] = jnp.swapaxes(speeds[:, b0:b1, at], 0, 1)

    def field(block, d, lanes):
        return (q0[block, :, lanes] * cs[block, d : d + 1, lanes],)

    pack(oc, sends, field, (up, dn))


def spread(capacity, packets, part, targets, sems):
    copies = []
    for side, packet in enumerate(packets):
        base = part * PACK
        slot = capacity + 4 * side
        pieces = (
            (0, 0, CELLS),
            (1, CELLS, XFACES - CELLS),
            (2, XFACES, CELLS),
            (3, XFACES + CELLS, CELLS),
        )
        for i, (sub, lane, width) in enumerate(pieces):
            target = targets[max(sub - 1, 0)]
            copies.append(
                pltpu.make_async_copy(
                    packet.at[:, pl.ds(base + lane, width)],
                    target.at[slot + sub, :, pl.ds(0, width)],
                    sems.at[4 * side + i],
                )
            )
    return copies


def sources(tab, b):
    at = T_SRC + 8 * b
    sx, tx, rx, sy, ry, sz, rz = [tab[at + i] for i in range(7)]
    return sx, pl.ds(pl.multiple_of(tx, TILE), TILE), rx, sy, ry, sz, rz


def first_kernel(capacity, tab, sends, q0, cs, from_prev, from_next, q1, up, dn, qx, cx, sem, sems):
    load = pltpu.make_async_copy(q0, qx.at[pl.ds(0, capacity)], sem)
    load.start()
    copies = spread(capacity, (from_prev, from_next), 0, (qx, qx, qx), sems)
    for copy in copies:
        copy.start()
    table = pltpu.make_async_copy(cs, cx.at[pl.ds(0, capacity)], sems.at[8])
    table.start()
    copies.append(table)
    for i in range(EXTRA):
        cx[capacity + i] = jnp.ones((3, CELLS), F32)
    for copy in copies:
        copy.wait()
    load.wait()
    low = low_half()
    y0, z0 = lane_coord(1) == 0, lane_coord(2) == 0
    oc = tab[T_OC]

    def step(b, carry):
        sx, tx, rx, sy, ry, sz, rz = sources(tab, b)
        before = None
        for t in range(TILES):
            at = pl.ds(t * TILE, TILE)
            c = [cx[b, d : d + 1, at] for d in range(3)]
            keep = 1.0 - c[0] - c[1] - c[2]
            cuy, cuz = cx[sy, 1:2, at], cx[sz, 2:3, at]
            if t == 0:
                cux = cx[sx, 0:1, tx]
            else:
                cm = jnp.where(low, c[0], before)
            for r0, r1 in ROWSETS:
                q = qx[b, r0:r1, at]
                if t == 0:
                    far = pltpu.roll(qx[sx, r0:r1, tx] * cux, rx, 1)
                    mixed = jnp.where(low, q * c[0], far)
                else:
                    mixed = jnp.where(low, q, qx[b, r0:r1, pl.ds((t - 1) * TILE, TILE)]) * cm
                inx = pltpu.roll(mixed, 64, 1)
                iny = jnp.where(
                    y0, pltpu.roll(qx[sy, r0:r1, at] * cuy, ry, 1), pltpu.roll(q * c[1], 8, 1)
                )
                inz = jnp.where(
                    z0, pltpu.roll(qx[sz, r0:r1, at] * cuz, rz, 1), pltpu.roll(q * c[2], 1, 1)
                )
                q1[b, r0:r1, at] = q * keep + (inx + (iny + inz))
            before = c[0]
        return carry

    lax.fori_loop(0, oc, step, 0)

    def field(block, d, lanes):
        q = q1[block, :, lanes]
        c = cx[block, d : d + 1, lanes]
        m = q - pltpu.roll(q, STRIDES[d], 1)
        m = jnp.maximum(jnp.minimum(m, q), 0.0)
        return c * q + (0.5 * c * (1.0 - c)) * m, q

    pack(oc, sends, field, (up, dn))


def second_kernel(
    capacity, tab, q1, cs, from_prev, from_next, q2out, *rest
):
    chunks = HALF // CHUNK
    ups, dns = rest[:chunks], rest[chunks : 2 * chunks]
    qx, fx, fy, fz, q2, sem, lsems, fsems, osems = rest[2 * chunks :]
    fluxes = (fx, fy, fz)
    packets = (from_prev, from_next)
    load = pltpu.make_async_copy(q1, qx.at[pl.ds(0, capacity)], sem)
    load.start()
    copies = spread(capacity, packets, 1, (qx, qx, qx), lsems)
    copies += spread(capacity, packets, 0, fluxes, fsems)
    for copy in copies:
        copy.start()
    for copy in copies:
        copy.wait()
    load.wait()
    low = low_half()
    y0, z0 = lane_coord(1) == 0, lane_coord(2) == 0
    oc = tab[T_OC]

    def limit(b, carry):
        sx, tx, rx, sy, ry, sz, rz = sources(tab, b)
        for t in range(TILES):
            at = pl.ds(t * TILE, TILE)
            c = [cs[b, d : d + 1, at] for d in range(3)]
            half = [0.5 * v * (1.0 - v) for v in c]
            for r0, r1 in ROWSETS:
                q = qx[b, r0:r1, at]
                if t == 0:
                    far = pltpu.roll(qx[sx, r0:r1, tx], rx, 1)
                else:
                    far = qx[b, r0:r1, pl.ds((t - 1) * TILE, TILE)]
                before = (
                    pltpu.roll(jnp.where(low, q, far), 64, 1),
                    jnp.where(y0, pltpu.roll(qx[sy, r0:r1, at], ry, 1), pltpu.roll(q, 8, 1)),
                    jnp.where(z0, pltpu.roll(qx[sz, r0:r1, at], rz, 1), pltpu.roll(q, 1, 1)),
                )
                rest = q
                for d in range(3):
                    m = jnp.maximum(jnp.minimum(q - before[d], q), 0.0)
                    flux = c[d] * q + half[d] * m
                    fluxes[d][b, r0:r1, at] = flux
                    rest = rest - flux
                q2[b, r0:r1, at] = rest
        return carry

    lax.fori_loop(0, oc, limit, 0)

    def step(b, carry):
        sx, tx, rx, sy, ry, sz, rz = sources(tab, b)
        for t in range(TILES):
            at = pl.ds(t * TILE, TILE)
            for r0, r1 in ROWSETS:
                if t == 0:
                    far = pltpu.roll(fx[sx, r0:r1, tx], rx, 1)
                else:
                    far = fx[b, r0:r1, pl.ds((t - 1) * TILE, TILE)]
                inx = pltpu.roll(jnp.where(low, fx[b, r0:r1, at], far), 64, 1)
                iny = jnp.where(
                    y0, pltpu.roll(fy[sy, r0:r1, at], ry, 1), pltpu.roll(fy[b, r0:r1, at], 8, 1)
                )
                inz = jnp.where(
                    z0, pltpu.roll(fz[sz, r0:r1, at], rz, 1), pltpu.roll(fz[b, r0:r1, at], 1, 1)
                )
                q2[b, r0:r1, at] = q2[b, r0:r1, at] + (inx + (iny + inz))
        return carry

    lax.fori_loop(0, oc, step, 0)
    outs = [pltpu.make_async_copy(q2, q2out, osems.at[0])]
    for c in range(chunks):
        outs.append(
            pltpu.make_async_copy(
                q2.at[pl.ds(oc - HALF + c * CHUNK, CHUNK)], ups[c], osems.at[1 + c]
            )
        )
        outs.append(
            pltpu.make_async_copy(
                q2.at[pl.ds(c * CHUNK, CHUNK)], dns[c], osems.at[1 + chunks + c]
            )
        )
    for copy in outs:
        copy.start()
    for copy in outs:
        copy.wait()


def build_pairs(q, qp, pairs):
    qp[0:BINS, :] = q
    qp[BINS:ROWS, :] = jnp.zeros((ROWS - BINS, CELLS), F32)
    pending = []

    def emit(term):
        pending.append(term)
        if len(pending) % 2 == 0:
            at = 8 * (len(pending) - 2)
            tile = jnp.concatenate(pending[-2:], axis=0)
            pairs[at : at + 16, :] = tile.astype(jnp.bfloat16)

    def lead(i):
        return jnp.broadcast_to(qp[i : i + 1, :], (8, CELLS))

    def group(g):
        return qp[8 * g : 8 * g + 8, :]

    for a in range(7):
        for r in range(8):
            by = lead(8 * a + r)
            for b in range(a + 1, 8):
                emit(by * group(b))
    for e in (BINS - 2, BINS - 1):
        by = lead(e)
        for a in range(8):
            emit(by * group(a))
    for a in range(8):
        g = group(a)
        emit(g * g)
        for k in range(1, 5):
            emit(g * pltpu.roll(g, 8 - k, 0))
    tail = group(8)
    emit(tail * tail)
    emit(lead(BINS - 1) * tail)
    while len(pending) < GROUPS:
        emit(jnp.zeros((8, CELLS), F32))


def coalesce(count, load, slot_of, w, out, qps, pairs, res, sems):
    def copy_out(slot, buf):
        return pltpu.make_async_copy(res.at[buf], out.at[slot], sems.at[buf])

    def body(it, carry):
        first = 2 * it
        items = (first, jnp.minimum(first + 1, count - 1))
        values = [load(i) for i in items]

        @pl.when(it > 0)
        def _():
            for buf in range(2):
                copy_out(0, buf).wait()

        for buf in range(2):
            build_pairs(values[buf], qps[buf], pairs[buf])
        for buf in range(2):
            gain = jnp.dot(w[...], pairs[buf][...], preferred_element_type=F32)
            res[buf] = qps[buf][0:BINS, :] + gain
        copy_out(slot_of(items[0]), 0).start()

        @pl.when(first + 1 < count)
        def _():
            copy_out(slot_of(items[1]), 1).start()

        return carry

    trips = lax.div(count + 1, 2)
    lax.fori_loop(0, trips, body, 0)

    @pl.when(trips > 0)
    def _():
        copy_out(0, 0).wait()

    @pl.when((trips > 0) & (lax.rem(count, 2) == 0))
    def _():
        copy_out(0, 1).wait()


def ranges(tab):
    oc, nc, old, new = tab[T_OC], tab[T_NC], tab[T_OS], tab[T_NS]
    lo = jnp.clip(old - new, 0, nc)
    hi = jnp.clip(old + oc - new, lo, nc)
    return lo, hi, nc, new - old


def stay_kernel(capacity, tab, q2, w, out, qpa, qpb, pa, pb, res, zero, sems, zsem):
    lo, hi, nc, shift = ranges(tab)
    zero[...] = jnp.zeros_like(zero)

    def blank(slot):
        return pltpu.make_async_copy(zero, out.at[slot], zsem)

    def start(slot, carry):
        blank(slot).start()
        return carry

    def wait(slot, carry):
        blank(slot).wait()
        return carry

    lax.fori_loop(nc, capacity, start, 0)
    coalesce(
        hi - lo,
        lambda i: q2[i + lo + shift],
        lambda i: i + lo,
        w,
        out,
        (qpa, qpb),
        (pa, pb),
        res,
        sems,
    )
    lax.fori_loop(nc, capacity, wait, 0)


def come_kernel(c, tab, from_prev, from_next, w, old_out, out, qpa, qpb, pa, pb, res, src, sems, lsems):
    lo, hi, nc, _ = ranges(tab)
    loads = [
        pltpu.make_async_copy(ref, src.at[pl.ds(side * CHUNK, CHUNK)], lsems.at[side])
        for side, ref in enumerate((from_prev, from_next))
    ]
    for copy in loads:
        copy.start()
    for copy in loads:
        copy.wait()
    skip = jnp.clip(HALF - lo - c * CHUNK, 0, CHUNK)
    ups = CHUNK - skip
    downs = jnp.clip(nc - hi - c * CHUNK, 0, CHUNK)
    slot_up = c * CHUNK + skip - HALF + lo
    slot_dn = hi + c * CHUNK
    coalesce(
        ups + downs,
        lambda i: src[jnp.where(i < ups, i + skip, i - ups + CHUNK)],
        lambda i: jnp.where(i < ups, i + slot_up, i - ups + slot_dn),
        w,
        out,
        (qpa, qpb),
        (pa, pb),
        res,
        sems,
    )


def folded_kernel(kernel):
    cube = kernel.reshape(BINS, BINS, BINS).astype(F32)
    both = cube + jnp.swapaxes(cube, 1, 2)
    a, b = BINS - 2, BINS - 1
    parts = [both[:, 8 * g : 8 * g + 8, 8 * g + 8 : a].reshape(BINS, -1) for g in range(7)]
    parts += [both[:, a, :a], both[:, b, :a]]
    s = lax.broadcasted_iota(jnp.int32, (1, 8, 8), 1)
    t = lax.broadcasted_iota(jnp.int32, (1, 8, 8), 2)
    for g in range(8):
        at = slice(8 * g, 8 * g + 8)
        for k in range(5):
            block = (both if 0 < k < 4 else cube)[:, at, at]
            parts.append(jnp.sum(jnp.where(t == (s + k) % 8, block, 0.0), axis=2))
    zero = jnp.zeros((BINS, 6), F32)
    parts += [cube[:, a, a][:, None], cube[:, b, b][:, None], zero]
    parts += [both[:, a, b][:, None], jnp.zeros((BINS, 7), F32)]
    width = sum(p.shape[1] for p in parts)
    parts.append(jnp.zeros((BINS, KDIM - width), F32))
    return jnp.concatenate([p.astype(jnp.bfloat16) for p in parts], axis=1)


def on_device(n, spectra, courant, kernel, old_count, new_count, upwind):
    capacity = spectra.shape[0]
    shape = jax.ShapeDtypeStruct
    vmem = pl.BlockSpec(memory_space=pltpu.VMEM)
    smem = pl.BlockSpec(memory_space=pltpu.SMEM)
    hbm = pl.BlockSpec(memory_space=pl.ANY)
    params = pltpu.CompilerParams(vmem_limit_bytes=VMEM_LIMIT)
    blocks = shape((capacity, BINS, CELLS), F32)
    chunk = shape((CHUNK, BINS, CELLS), F32)
    chunks = HALF // CHUNK
    wide = pltpu.VMEM((capacity + EXTRA, BINS, CELLS), F32)
    dma = pltpu.SemaphoreType.DMA

    def cost(flops, nbytes):
        return pl.CostEstimate(flops=flops, bytes_accessed=nbytes, transcendentals=0)

    upw = jnp.swapaxes(upwind, 0, 1)
    sends, up, dn, cs = pl.pallas_call(
        functools.partial(faces_kernel, n, capacity),
        out_shape=(
            shape((S_LIST + 32,), jnp.int32),
            shape((BINS, PACK), F32),
            shape((BINS, PACK), F32),
            shape((capacity, 3, CELLS), F32),
        ),
        in_specs=[smem, smem, smem, vmem, vmem],
        out_specs=(smem, vmem, vmem, vmem),
        compiler_params=params,
        name="faces",
    )(old_count, new_count, upw, spectra, jnp.swapaxes(courant, 0, 1))

    def along(value, step, ring):
        route = [(i, i + step) for i in range(n)]
        if ring:
            route = [(i, j % n) for i, j in route]
        return lax.ppermute(value, "blocks", [(i, j) for i, j in route if 0 <= j < n])

    from_prev, from_next = along(up, 1, True), along(dn, -1, True)
    tab = pl.pallas_call(
        functools.partial(plan_kernel, n, capacity),
        out_shape=shape((T_SRC + 8 * capacity,), jnp.int32),
        in_specs=[smem] * 4,
        out_specs=smem,
        cost_estimate=cost(1000000, 1000000),
        name="plan",
    )(sends, old_count, new_count, upw)
    weights = folded_kernel(kernel)
    packed = shape((BINS, 2 * PACK), F32)
    q1, up, dn = pl.pallas_call(
        functools.partial(first_kernel, capacity),
        out_shape=(blocks, packed, packed),
        in_specs=[smem, smem, hbm, hbm, hbm, hbm],
        out_specs=(vmem, vmem, vmem),
        scratch_shapes=[
            wide,
            pltpu.VMEM((capacity + EXTRA, 3, CELLS), F32),
            dma,
            dma((9,)),
        ],
        compiler_params=params,
        name="first",
    )(tab, sends, spectra, cs, from_prev, from_next)
    from_prev, from_next = along(up, 1, True), along(dn, -1, True)
    q1, weights = lax.optimization_barrier((q1, weights))
    q2, *moved = pl.pallas_call(
        functools.partial(second_kernel, capacity),
        out_shape=[blocks] + [chunk] * (2 * chunks),
        in_specs=[smem, hbm, vmem, hbm, hbm],
        out_specs=[hbm] * (1 + 2 * chunks),
        scratch_shapes=[
            wide,
            wide,
            wide,
            wide,
            pltpu.VMEM((capacity, BINS, CELLS), F32),
            dma,
            dma((8,)),
            dma((8,)),
            dma((1 + 2 * chunks,)),
        ],
        compiler_params=params,
        name="second",
    )(tab, q1, cs, from_prev, from_next)
    arrived = [
        (along(moved[c], 1, False), along(moved[chunks + c], -1, False)) for c in range(chunks)
    ]
    buffers = [
        pltpu.VMEM((ROWS, CELLS), F32),
        pltpu.VMEM((ROWS, CELLS), F32),
        pltpu.VMEM((KDIM, CELLS), jnp.bfloat16),
        pltpu.VMEM((KDIM, CELLS), jnp.bfloat16),
        pltpu.VMEM((2, BINS, CELLS), F32),
    ]
    work = 2 * BINS * KDIM * CELLS
    updated = pl.pallas_call(
        functools.partial(stay_kernel, capacity),
        out_shape=blocks,
        in_specs=[smem, vmem, vmem],
        out_specs=hbm,
        scratch_shapes=buffers + [pltpu.VMEM((BINS, CELLS), F32), dma((2,)), dma],
        compiler_params=params,
        cost_estimate=cost(24 * work, 12 * 1024 * 1024),
        name="stay",
    )(tab, q2, weights)
    for c in range(chunks):
        updated = pl.pallas_call(
            functools.partial(come_kernel, c),
            out_shape=blocks,
            in_specs=[smem, hbm, hbm, vmem, hbm],
            out_specs=hbm,
            input_output_aliases={4: 0},
            scratch_shapes=buffers
            + [pltpu.VMEM((2 * CHUNK, BINS, CELLS), F32), dma((2,)), dma((2,))],
            compiler_params=params,
            cost_estimate=cost(8 * work, 4 * 1024 * 1024),
            name=f"come{c}",
        )(tab, *arrived[c], weights, updated)
    return updated


def solution(mesh):
    in_specs = (P("blocks", None, None), P("blocks", None, None), P(), P(), P(), P())
    out_specs = P("blocks", None, None)
    return jax.shard_map(
        functools.partial(on_device, mesh.shape["blocks"]),
        mesh=mesh,
        in_specs=in_specs,
        out_specs=out_specs,
        check_vma=False,
    )
```

time: 191 us -> 178 us (0.932)
  the two profiles are of different devices: /device:TPU:4 before, /device:TPU:3 now
where the time goes in v1:
time: 178 us; the launch traced here: 176 us
  Pallas kernels  85 us (48%)
  local copies, waits for them, and re-layouts  37.3 us (21%)
  starting transfers between devices  33.1 us (19%)
  other arithmetic  14.3 us (8%)
  waiting for transfers between devices  5.37 us (3%)
    ppermute x10, starting transfers between devices, along(): lax.ppermute(value, 'blocks', [(i, j) for i, j in route if 0 <= j < n])  33.1 us
    pallas_call x1, Pallas kernels, on_device(): pl.pallas_call(functools.partial(stay_kernel, capacity), out_shape=blocks...  22.9 us
    pallas_call x1, Pallas kernels, on_device(): pl.pallas_call(functools.partial(second_kernel, capacity), out_shape=[blo...  22.5 us
    pallas_call x3, Pallas kernels, on_device(): pl.pallas_call(functools.partial(come_kernel, c), out_shape=blocks, in_sp...  17 us
    pallas_call x1, Pallas kernels, on_device(): pl.pallas_call(functools.partial(first_kernel, capacity), out_shape=(bloc...  15.1 us
    ppermute x6, local copies, waits for them, and re-layouts, along(): lax.ppermute(value, 'blocks', [(i, j) for i, j in route if 0 <= j < n])  12.3 us
    reduce_sum x2, other arithmetic, folded_kernel(): parts.append(jnp.sum(jnp.where(t == (s + k) % 8, block, 0.0), axis=2))  8.3 us
    pallas_call x6, local copies, waits for them, and re-layouts, on_device(): pl.pallas_call(functools.partial(second_kernel, capacity), out_shape=[blo...  7.63 us
  transfers between devices with their start and end apart: 10, of which 2 were waited for; matrix products, arithmetic and copies ran while one was open for 27% of the time, Pallas kernels for 21%

profile of v1, /device:TPU:3, one launch (start us, length us, event | category | flops | bytes accessed | tf_op | source)
XLA Modules:
  0.0 175.8 jit_solution(232973942927243390)
XLA Ops:
  0.0 4.8 %faces.1 = (s32[40]{0:T(128)}, f32[66,1792]{1,0:T(8,128)}, f32[66,1792]{1,0:T(8,128)}, f32[36,3,512]{2,1,0:T(4,128)}) custom-call(s32[32]{0:T(128)} %old.3, s32[32]{0:T(128)} %new.3, s32[3,768]{1,0:T(4,128)} %bitcast.25, f32[36,66,512]{2,1,0:T(8,128)} %q0.3, f32[3,36,512]{2,1,0:T(8,128)} %bitcast.21), custom_call_target="tpu_custom_call" | custom-call | tf_op jit(solution)/shard_map/faces/pallas_call | solution.py:545
  4.8 1.8 %collective-permute-start = (f32[66,1792]{1,0:T(8,128)}, f32[66,1792]{1,0:T(8,128)}, u32[]{:S(2)}, u32[]{:S(2)}) collective-permute-start(f32[66,1792]{1,0:T(8,128)} %get-tuple-element.23), channel_id=1, source_target_pairs={{0,1},{1,2},{2,3},{3,4},{4,5},{5,6},{6,7},{7,8},{8,9},{9,10},{10,1... | collective-permute-start | bytes 1419272 | tf_op jit(solution)/shard_map/ppermute | solution.py:563
  6.7 1.1 convert_element_type.207
  7.9 2.8 %plan.1.tab = s32[296]{0:T(512)} custom-call(s32[40]{0:T(128)} %get-tuple-element.21.sends, s32[32]{0:T(128)} %old.3, s32[32]{0:T(128)} %new.3, s32[3,768]{1,0:T(4,128)} %bitcast.26), custom_call_target="tpu_custom_call" | custom-call | flops 1000000 | bytes 1000000 | tf_op jit(solution)/shard_map/plan/pallas_call | solution.py:566
  10.7 2.5 %copy_convert_fusion = (f32[66,66,66]{2,0,1:T(8,128)}, f32[66,66,66]{1,0,2:T(8,128)}) fusion(bf16[66,66,66]{2,1,0:T(8,128)(2,1)S(1)} %convert_element_type.207), kind=kLoop, calls=%fused_computation | loop fusion | flops 287496 | bytes 2874960 | tf_op jit(solution)/shard_map/convert_element_type | solution.py:508
  13.3 3.5 %copy.32 = f32[66,66,66]{2,0,1:T(8,128)} copy(f32[66,66,66]{1,0,2:T(8,128)} %get-tuple-element.106) | data formatting | bytes 2299968 | tf_op jit(solution)/shard_map/transpose | solution.py:509
  16.7 3.1 %fusion.6 = (bf16[66,66,66]{2,0,1:T(8,128)(2,1)}, f32[66,66,66]{2,0,1:T(8,128)S(1)}) fusion(f32[66,66,66]{2,0,1:T(8,128)} %copy.32, bf16[66,66,66]{2,1,0:T(8,128)(2,1)S(1)} %convert_element_type.207), kind=kLoop, calls=%fused_computation.76 | loop fusion | flops 862488 | bytes 3449952 | tf_op jit(solution)/shard_map/convert.12
  20.2 3.9 %select_reduce_fusion.1 = (bf16[66,8]{0,1:T(8,128)(2,1)S(1)}, bf16[66,8]{0,1:T(8,128)(2,1)S(1)}, bf16[66,8]{0,1:T(8,128)(2,1)S(1)}, bf16[66,8]{0,1:T(8,128)(2,1)...) fusion(f32[66,66,66]{2,0,1:T(8,128)S(1)} %get-tuple-element.94,, ...), kind=kLoop, calls=%fused_computation.4 | loop fusion | flops 190080 | bytes 160704 | tf_op jit(solution)/shard_map/reduce_sum | solution.py:519
  24.1 15.1 %first.1 = (f32[36,66,512]{2,1,0:T(8,128)}, f32[66,3584]{1,0:T(8,128)}, f32[66,3584]{1,0:T(8,128)}) custom-call(s32[296]{0:T(512)} %plan.1.tab, s32[40]{0:T(128)} %get-tuple-element.21.sends, f32[36,66,512]{2,1,0:T(8,128)} %q0.3, f32[36,3,512]{2,1,0:T(4,128)} %get-tuple-element.22.cs, f32[66,1792]{1,0:T(8,128)} %collective-permute-done.from_prev, ...), custom_call_target="tpu_custom_call" | custom-call | tf_op jit(solution)/shard_map/first/pallas_call | solution.py:576
  39.2 2.7 %collective-permute-start.2 = (f32[66,3584]{1,0:T(8,128)}, f32[66,3584]{1,0:T(8,128)}, u32[]{:S(2)}, u32[]{:S(2)}) collective-permute-start(f32[66,3584]{1,0:T(8,128)} %get-tuple-element.27), channel_id=1, source_target_pairs={{0,1},{1,2},{2,3},{3,4},{4,5},{5,6},{6,7},{7,8},{8,9},{9,10},{10,1... | collective-permute-start | bytes 2838536 | tf_op jit(solution)/shard_map/ppermute | solution.py:563
  41.9 1.9 %collective-permute-start.3 = (f32[66,3584]{1,0:T(8,128)}, f32[66,3584]{1,0:T(8,128)}, u32[]{:S(2)}, u32[]{:S(2)}) collective-permute-start(f32[66,3584]{1,0:T(8,128)} %get-tuple-element.28), channel_id=1, source_target_pairs={{0,31},{1,0},{2,1},{3,2},{4,3},{5,4},{6,5},{7,6},{8,7},{9,8},{10,9... | collective-permute-start | bytes 2838536 | tf_op jit(solution)/shard_map/ppermute | solution.py:563
  43.8 4.4 %select_reduce_fusion = (bf16[66,8]{0,1:T(8,128)(2,1)S(1)}, bf16[66,8]{0,1:T(8,128)(2,1)S(1)}, bf16[66,8]{0,1:T(8,128)(2,1)S(1)}, bf16[66,8]{0,1:T(8,128)(2,1)S(...) fusion(f32[66,66,66]{2,0,1:T(8,128)} %get-tuple-element.105, ...), kind=kLoop, calls=%fused_computation.3 | loop fusion | flops 126720 | bytes 152192 | tf_op jit(solution)/shard_map/reduce_sum | solution.py:519
  49.7 0.1 copy.74
  50.0 0.1 copy.45
  50.1 0.1 copy.50
  50.5 0.1 copy.65
  50.6 0.1 copy.70
  51.0 0.1 copy.48
  51.1 0.1 copy.53
  51.4 0.1 copy.68
  51.6 0.1 copy.73
  51.9 0.1 copy.72
  52.0 0.1 copy.67
  52.4 0.1 copy.52
  52.5 0.1 copy.47
  52.8 0.1 copy.51
  53.0 0.1 copy.56
  53.3 0.1 copy.71
  53.4 0.1 copy.76
  53.7 0.1 copy.39
  53.9 0.1 copy.38
  54.2 0.1 copy.37
  54.4 0.1 copy.36
  54.7 0.1 copy.35
  54.8 0.1 copy.40
  55.0 0.1 convert_element_type.209
  55.2 0.2 convert_element_type.210
  55.4 1.1 fusion.8
  56.6 4.5 %concatenate.3.w = bf16[66,2304]{1,0:T(8,128)(2,1)} concatenate(bf16[66,448]{1,0:T(8,128)(2,1)S(1)} %convert_element_type.209, bf16[66,384]{1,0:T(8,128)(2,1)S(1)} %convert_element_type.210, bf16[66,320]{1,0:T(8,128)(2,1)S(1)} %copy.40, bf16[66,256]{1,0:T(8,128)(2,1)S(1)} %copy.41, bf16[66,192]{1,0:T(8,128)(2,1)S(1)} %copy.42, bf16[66,128]{1,0:T(8,128)(2,1)S(1)} %copy.43, ...), dimensions={1} | concatenate | bytes 608256 | tf_op jit(solution)/shard_map/concatenate | solution.py:525
  61.1 0.2 collective-permute-done.2.from_prev
  61.3 5.2 %collective-permute-done.3.from_next = f32[66,3584]{1,0:T(8,128)} collective-permute-done((f32[66,3584]{1,0:T(8,128)}, f32[66,3584]{1,0:T(8,128)}, u32[]{:S(2)}, u32[]{:S(2)}) %collective-permute-start.3) | collective-permute-done | bytes 946208 | tf_op jit(solution)/shard_map/ppermute | solution.py:563
  66.5 22.5 %second.1 = (f32[36,66,512]{2,1,0:T(8,128)}, f32[4,66,512]{2,1,0:T(8,128)}, f32[4,66,512]{2,1,0:T(8,128)}, f32[4,66,512]{2,1,0:T(8,128)}, f32[4,66,512]{2,1,0:T(...) custom-call(s32[296]{0:T(512)} %plan.1.tab, f32[36,66,512]{2,1,0:T(8,128)} %get-tuple-element.26.q1, ...), custom_call_target="tpu_custom_call" | custom-call | tf_op jit(solution)/shard_map/second/pallas_call | solution.py:592
  89.0 1.5 copy.93
  90.5 11.9 %collective-permute-start.9 = (f32[4,66,512]{2,0,1:T(4,128)S(1)}, f32[4,66,512]{2,0,1:T(4,128)}, u32[]{:S(2)}, u32[]{:S(2)}) collective-permute-start(f32[4,66,512]{2,0,1:T(4,128)S(1)} %copy.93), channel_id=1, source_target_pairs={{1,0},{2,1},{3,2},{4,3},{5,4},{6,5},{7,6},{8,7},{9,8},{10,9},{11,1... | collective-permute-start | bytes 1622024 | tf_op jit(solution)/shard_map/ppermute | solution.py:563
  102.4 1.4 copy.90
  103.8 1.2 copy.92
  105.0 1.9 %collective-permute-start.8 = (f32[4,66,512]{2,0,1:T(4,128)}, f32[4,66,512]{2,0,1:T(4,128)}, u32[]{:S(2)}, u32[]{:S(2)}) collective-permute-start(f32[4,66,512]{2,0,1:T(4,128)} %copy.92), channel_id=1, source_target_pairs={{0,1},{1,2},{2,3},{3,4},{4,5},{5,6},{6,7},{7,8},{8,9},{9,10},{10,1... | collective-permute-start | bytes 1622024 | tf_op jit(solution)/shard_map/ppermute | solution.py:563
  106.9 1.2 copy.91
  108.1 2.4 %collective-permute-start.7 = (f32[4,66,512]{2,0,1:T(4,128)}, f32[4,66,512]{2,0,1:T(4,128)}, u32[]{:S(2)}, u32[]{:S(2)}) collective-permute-start(f32[4,66,512]{2,0,1:T(4,128)} %copy.91), channel_id=1, source_target_pairs={{1,0},{2,1},{3,2},{4,3},{5,4},{6,5},{7,6},{8,7},{9,8},{10,9},{11,1... | collective-permute-start | bytes 1622024 | tf_op jit(solution)/shard_map/ppermute | solution.py:563
  110.5 4.1 %collective-permute-start.6 = (f32[4,66,512]{2,0,1:T(4,128)S(1)}, f32[4,66,512]{2,0,1:T(4,128)}, u32[]{:S(2)}, u32[]{:S(2)}) collective-permute-start(f32[4,66,512]{2,0,1:T(4,128)S(1)} %copy.90), channel_id=1, source_target_pairs={{0,1},{1,2},{2,3},{3,4},{4,5},{5,6},{6,7},{7,8},{8,9},{9,10},{10,1... | collective-permute-start | bytes 1622024 | tf_op jit(solution)/shard_map/ppermute | solution.py:563
  114.6 1.2 copy.89
  115.8 1.9 %collective-permute-start.5 = (f32[4,66,512]{2,0,1:T(4,128)}, f32[4,66,512]{2,0,1:T(4,128)}, u32[]{:S(2)}, u32[]{:S(2)}) collective-permute-start(f32[4,66,512]{2,0,1:T(4,128)} %copy.89), channel_id=1, source_target_pairs={{1,0},{2,1},{3,2},{4,3},{5,4},{6,5},{7,6},{8,7},{9,8},{10,9},{11,1... | collective-permute-start | bytes 1622024 | tf_op jit(solution)/shard_map/ppermute | solution.py:563
  117.7 1.1 copy.88
  118.8 4.5 %collective-permute-start.4 = (f32[4,66,512]{2,0,1:T(4,128)}, f32[4,66,512]{2,0,1:T(4,128)}, u32[]{:S(2)}, u32[]{:S(2)}) collective-permute-start(f32[4,66,512]{2,0,1:T(4,128)} %copy.88), channel_id=1, source_target_pairs={{0,1},{1,2},{2,3},{3,4},{4,5},{5,6},{6,7},{7,8},{8,9},{9,10},{10,1... | collective-permute-start | bytes 1622024 | tf_op jit(solution)/shard_map/ppermute | solution.py:563
  123.4 22.9 %stay.1.old_out = f32[36,66,512]{2,1,0:T(8,128)} custom-call(s32[296]{0:T(512)} %plan.1.tab, f32[36,66,512]{2,1,0:T(8,128)} %get-tuple-element.36.q2, bf16[66,2304]{1,0:T(8,128)(2,1)} %concatenate.3.w), custom_call_target="tpu_custom_call" | custom-call | flops 3737124864 | bytes 12582912 | tf_op jit(solution)/shard_map/stay/pallas_call | solution.py:622
  146.3 2.0 %copy.95.from_next = f32[4,66,512]{2,1,0:T(8,128)} copy(f32[4,66,512]{2,0,1:T(4,128)} %collective-permute-done.9) | data formatting | bytes 1081344 | tf_op jit(solution)/shard_map/ppermute | solution.py:563
  148.4 2.1 %copy.94.from_prev = f32[4,66,512]{2,1,0:T(8,128)} copy(f32[4,66,512]{2,0,1:T(4,128)} %collective-permute-done.8) | data formatting | bytes 1081344 | tf_op jit(solution)/shard_map/ppermute | solution.py:563
  150.4 2.1 %copy.97.from_next = f32[4,66,512]{2,1,0:T(8,128)} copy(f32[4,66,512]{2,0,1:T(4,128)} %collective-permute-done.7) | data formatting | bytes 1081344 | tf_op jit(solution)/shard_map/ppermute | solution.py:563
  152.5 2.0 %copy.96.from_prev = f32[4,66,512]{2,1,0:T(8,128)} copy(f32[4,66,512]{2,0,1:T(4,128)} %collective-permute-done.6) | data formatting | bytes 1081344 | tf_op jit(solution)/shard_map/ppermute | solution.py:563
  154.5 2.0 %copy.99.from_next = f32[4,66,512]{2,1,0:T(8,128)} copy(f32[4,66,512]{2,0,1:T(4,128)} %collective-permute-done.5) | data formatting | bytes 1081344 | tf_op jit(solution)/shard_map/ppermute | solution.py:563
  156.6 5.7 %come0.1.old_out = f32[36,66,512]{2,1,0:T(8,128)} custom-call(s32[296]{0:T(512)} %plan.1.tab, f32[4,66,512]{2,1,0:T(8,128)} %copy.94.from_prev, f32[4,66,512]{2,1,0:T(8,128)} %copy.95.from_next, bf16[66,2304]{1,0:T(8,128)(2,1)} %concatenate.3.w, f32[36,66,512]{2,1,0:T(8,128)} %stay.1.old_out), custom_call_target="tpu_custom_call", output_to_operand_aliasing={{}: (4, {})} | custom-call | flops 1245708288 | bytes 4194304 | tf_op jit(solution)/shard_map/come0/pallas_call | solution.py:633
  162.2 5.7 %come1.1.old_out = f32[36,66,512]{2,1,0:T(8,128)} custom-call(s32[296]{0:T(512)} %plan.1.tab, f32[4,66,512]{2,1,0:T(8,128)} %copy.96.from_prev, f32[4,66,512]{2,1,0:T(8,128)} %copy.97.from_next, bf16[66,2304]{1,0:T(8,128)(2,1)} %concatenate.3.w, f32[36,66,512]{2,1,0:T(8,128)} %come0.1.old_out), custom_call_target="tpu_custom_call", output_to_operand_aliasing={{}: (4, {})} | custom-call | flops 1245708288 | bytes 4194304 | tf_op jit(solution)/shard_map/come1/pallas_call | solution.py:633
  167.9 2.0 %copy.98.from_prev = f32[4,66,512]{2,1,0:T(8,128)} copy(f32[4,66,512]{2,0,1:T(4,128)} %collective-permute-done.4) | data formatting | bytes 1081344 | tf_op jit(solution)/shard_map/ppermute | solution.py:563
  170.0 5.7 %come2.1 = f32[36,66,512]{2,1,0:T(8,128)} custom-call(s32[296]{0:T(512)} %plan.1.tab, f32[4,66,512]{2,1,0:T(8,128)} %copy.98.from_prev, f32[4,66,512]{2,1,0:T(8,128)} %copy.99.from_next, bf16[66,2304]{1,0:T(8,128)(2,1)} %concatenate.3.w, f32[36,66,512]{2,1,0:T(8,128)} %come1.1.old_out), custom_call_target="tpu_custom_call", output_to_operand_aliasing={{}: (4, {})} | custom-call | flops 1245708288 | bytes 4194304 | tf_op jit(solution)/shard_map/come2/pallas_call | solution.py:633
  (80 shorter events, 4.5 us)
Async XLA Ops:
  0.0 6.7 %copy-start.2 = (bf16[66,4356]{1,0:T(8,128)(2,1)S(1)}, bf16[66,4356]{1,0:T(8,128)(2,1)}, u32[]{:S(2)}) copy-start(bf16[66,4356]{1,0:T(8,128)(2,1)} %param.8) | copy-start | bytes 1724980
  4.8 19.3 %collective-permute-start = (f32[66,1792]{1,0:T(8,128)}, f32[66,1792]{1,0:T(8,128)}, u32[]{:S(2)}, u32[]{:S(2)}) collective-permute-start(f32[66,1792]{1,0:T(8,128)} %get-tuple-element.23), channel_id=1, source_target_pairs={{0,1},{1,2},{2,3},{3,4},{4,5},{5,6},{6,7},{7,8},{8,9},{9,10},{10,1... | collective-permute-start | bytes 1419272 | tf_op jit(solution)/shard_map/ppermute | solution.py:563
  6.6 17.5 %collective-permute-start.1 = (f32[66,1792]{1,0:T(8,128)}, f32[66,1792]{1,0:T(8,128)}, u32[]{:S(2)}, u32[]{:S(2)}) collective-permute-start(f32[66,1792]{1,0:T(8,128)} %get-tuple-element.24), channel_id=1, source_target_pairs={{0,31},{1,0},{2,1},{3,2},{4,3},{5,4},{6,5},{7,6},{8,7},{9,8},{10,9... | collective-permute-start | bytes 1419272 | tf_op jit(solution)/shard_map/ppermute | solution.py:563
  7.9 8.8 %copy-start = (bf16[66,66,66]{2,1,0:T(8,128)(2,1)}, bf16[66,66,66]{2,1,0:T(8,128)(2,1)S(1)}, u32[]{:S(2)}) copy-start(bf16[66,66,66]{2,1,0:T(8,128)(2,1)S(1)} %convert_element_type.207) | copy-start | bytes 1724980
  39.2 9.0 %copy-start.1 = (bf16[66,66,66]{2,0,1:T(8,128)(2,1)S(1)}, bf16[66,66,66]{2,0,1:T(8,128)(2,1)}, u32[]{:S(2)}) copy-start(bf16[66,66,66]{2,0,1:T(8,128)(2,1)} %get-tuple-element.93) | copy-start | bytes 1724980
  39.2 22.1 %collective-permute-start.2 = (f32[66,3584]{1,0:T(8,128)}, f32[66,3584]{1,0:T(8,128)}, u32[]{:S(2)}, u32[]{:S(2)}) collective-permute-start(f32[66,3584]{1,0:T(8,128)} %get-tuple-element.27), channel_id=1, source_target_pairs={{0,1},{1,2},{2,3},{3,4},{4,5},{5,6},{6,7},{7,8},{8,9},{9,10},{10,1... | collective-permute-start | bytes 2838536 | tf_op jit(solution)/shard_map/ppermute | solution.py:563
  41.9 24.5 %collective-permute-start.3 = (f32[66,3584]{1,0:T(8,128)}, f32[66,3584]{1,0:T(8,128)}, u32[]{:S(2)}, u32[]{:S(2)}) collective-permute-start(f32[66,3584]{1,0:T(8,128)} %get-tuple-element.28), channel_id=1, source_target_pairs={{0,31},{1,0},{2,1},{3,2},{4,3},{5,4},{6,5},{7,6},{8,7},{9,8},{10,9... | collective-permute-start | bytes 2838536 | tf_op jit(solution)/shard_map/ppermute | solution.py:563
  88.9 14.9 %copy-start.6 = (f32[4,66,512]{2,1,0:T(8,128)S(1)}, f32[4,66,512]{2,1,0:T(8,128)}, u32[]{:S(2)}) copy-start(f32[4,66,512]{2,1,0:T(8,128)} %get-tuple-element.34) | copy-start | bytes 1622020
  88.9 18.0 %copy-start.5 = (f32[4,66,512]{2,1,0:T(8,128)S(1)}, f32[4,66,512]{2,1,0:T(8,128)}, u32[]{:S(2)}) copy-start(f32[4,66,512]{2,1,0:T(8,128)} %get-tuple-element.33) | copy-start | bytes 1622020
  89.0 25.6 %copy-start.4 = (f32[4,66,512]{2,1,0:T(8,128)S(1)}, f32[4,66,512]{2,1,0:T(8,128)}, u32[]{:S(2)}) copy-start(f32[4,66,512]{2,1,0:T(8,128)} %get-tuple-element.30) | copy-start | bytes 1622020
  90.5 27.2 %copy-start.3 = (f32[4,66,512]{2,1,0:T(8,128)S(1)}, f32[4,66,512]{2,1,0:T(8,128)}, u32[]{:S(2)}) copy-start(f32[4,66,512]{2,1,0:T(8,128)} %get-tuple-element.29) | copy-start | bytes 1622020
  90.5 28.3 %collective-permute-start.9 = (f32[4,66,512]{2,0,1:T(4,128)S(1)}, f32[4,66,512]{2,0,1:T(4,128)}, u32[]{:S(2)}, u32[]{:S(2)}) collective-permute-start(f32[4,66,512]{2,0,1:T(4,128)S(1)} %copy.93), channel_id=1, source_target_pairs={{1,0},{2,1},{3,2},{4,3},{5,4},{6,5},{7,6},{8,7},{9,8},{10,9},{11,1... | collective-permute-start | bytes 1622024 | tf_op jit(solution)/shard_map/ppermute | solution.py:563
  105.0 43.4 %collective-permute-start.8 = (f32[4,66,512]{2,0,1:T(4,128)}, f32[4,66,512]{2,0,1:T(4,128)}, u32[]{:S(2)}, u32[]{:S(2)}) collective-permute-start(f32[4,66,512]{2,0,1:T(4,128)} %copy.92), channel_id=1, source_target_pairs={{0,1},{1,2},{2,3},{3,4},{4,5},{5,6},{6,7},{7,8},{8,9},{9,10},{10,1... | collective-permute-start | bytes 1622024 | tf_op jit(solution)/shard_map/ppermute | solution.py:563
  108.1 42.3 %collective-permute-start.7 = (f32[4,66,512]{2,0,1:T(4,128)}, f32[4,66,512]{2,0,1:T(4,128)}, u32[]{:S(2)}, u32[]{:S(2)}) collective-permute-start(f32[4,66,512]{2,0,1:T(4,128)} %copy.91), channel_id=1, source_target_pairs={{1,0},{2,1},{3,2},{4,3},{5,4},{6,5},{7,6},{8,7},{9,8},{10,9},{11,1... | collective-permute-start | bytes 1622024 | tf_op jit(solution)/shard_map/ppermute | solution.py:563
  110.5 42.0 %collective-permute-start.6 = (f32[4,66,512]{2,0,1:T(4,128)S(1)}, f32[4,66,512]{2,0,1:T(4,128)}, u32[]{:S(2)}, u32[]{:S(2)}) collective-permute-start(f32[4,66,512]{2,0,1:T(4,128)S(1)} %copy.90), channel_id=1, source_target_pairs={{0,1},{1,2},{2,3},{3,4},{4,5},{5,6},{6,7},{7,8},{8,9},{9,10},{10,1... | collective-permute-start | bytes 1622024 | tf_op jit(solution)/shard_map/ppermute | solution.py:563
  115.8 38.8 %collective-permute-start.5 = (f32[4,66,512]{2,0,1:T(4,128)}, f32[4,66,512]{2,0,1:T(4,128)}, u32[]{:S(2)}, u32[]{:S(2)}) collective-permute-start(f32[4,66,512]{2,0,1:T(4,128)} %copy.89), channel_id=1, source_target_pairs={{1,0},{2,1},{3,2},{4,3},{5,4},{6,5},{7,6},{8,7},{9,8},{10,9},{11,1... | collective-permute-start | bytes 1622024 | tf_op jit(solution)/shard_map/ppermute | solution.py:563
  118.8 49.1 %collective-permute-start.4 = (f32[4,66,512]{2,0,1:T(4,128)}, f32[4,66,512]{2,0,1:T(4,128)}, u32[]{:S(2)}, u32[]{:S(2)}) collective-permute-start(f32[4,66,512]{2,0,1:T(4,128)} %copy.88), channel_id=1, source_target_pairs={{0,1},{1,2},{2,3},{3,4},{4,5},{5,6},{6,7},{7,8},{8,9},{9,10},{10,1... | collective-permute-start | bytes 1622024 | tf_op jit(solution)/shard_map/ppermute | solution.py:563
